TPU v7x, 1024 devices: a whole 8x8x8 slice. The times are simulated.
1024 devices in a mesh: dp: 16 (over x_hi, z), shard: 64 (over x_lo, y, core).
Axes of the slice: x: 8 (x_hi: 2, x_lo: 4; x = x_hi * 4 + x_lo), y: 8, z: 8, core: 2. Of those that a mesh axis runs over, the one named last changes fastest.
Arguments:
- head_terms: bfloat16 [2048, 64, 256], P('dp', 'shard'), may hold values from -0.1875 to 0.1875
- inputs: bfloat16 [2048, 2, 4096], P('dp'), may hold values from -6 to 6
- owner_list: int32 [64, 256, 1], P('shard'), may hold values from 0 to 15; in each aligned block of 16 rows (0 to 15, 16 to 31, ..., all dimensions but the last counted through in order) at most 2 rows name the same one
- param_slots: bfloat16 [64, 512, 4096], P('shard', 'dp'), may hold values from -3 to 3
- row_state: float32 [64, 512], P('shard', 'dp'), may hold values from 0.25 to 4
- col_state: float32 [64, 4, 4096], P('shard'), may hold values from 0.25 to 4
Outputs:
- new_params: bfloat16 [64, 512, 4096], P('shard', 'dp')
- new_rows: float32 [64, 512], P('shard', 'dp')
- new_cols: float32 [64, 4, 4096], P('shard')
Inputs may be any that keep to these rules, and one draw needn't show every extreme that they name: `owner_list`: each head's 256 rows fall into 16 aligned home blocks of 16 rows; within one home block no owner index is named more than 2 times.
All inputs are finite; a program needn't handle non-finite values.
Results may differ from a plain program's by a relative error of at most 0.0012.
Values sent between devices are 32-bit elements; how exact they have to be, the bound alone decides.
A program may use at most 64 MiB of HBM per device.

v0:
```python
import jax
import jax.numpy as jnp
from jax import lax
from jax.sharding import PartitionSpec as P

DKV = 64
PROJ = 4


DECAY_RATE = 0.5
STEP_SIZE = 0.5
EPS_SQUARE = 1e-30


def slot_table(owner_col, owner_count, pair_most):
    row_count = owner_col.shape[0]
    block_rows = row_count // owner_count
    index_ids = jnp.arange(owner_count, dtype=jnp.int32)
    onehot = (owner_col[:, None] == index_ids[None, :]).astype(jnp.int32)
    blocked = onehot.reshape(owner_count, block_rows, owner_count)
    before = jnp.cumsum(blocked, axis=1) - blocked
    order_in = jnp.sum(before * blocked, axis=2).reshape(row_count)
    row_ids = jnp.arange(row_count, dtype=jnp.int32)
    block_of = row_ids // block_rows
    slot_ids = jnp.arange(pair_most, dtype=jnp.int32)
    match_owner = owner_col[None, None, None, :] == index_ids[:, None, None, None]
    match_block = block_of[None, None, None, :] == index_ids[None, :, None, None]
    match_slot = order_in[None, None, None, :] == slot_ids[None, None, :, None]
    hits = (match_owner & match_block & match_slot).astype(jnp.int32)
    live_mask = jnp.sum(hits, axis=3).reshape(owner_count, owner_count * pair_most)
    slot_row = jnp.sum(hits * row_ids[None, None, None, :], axis=3).reshape(
        owner_count, owner_count * pair_most
    )
    return (slot_row, live_mask)


def on_device(head_terms, inputs, owner_list, param_slots, row_state, col_state):
    dp_count = lax.axis_size("dp")
    my_index = lax.axis_index("dp")
    head_rows = head_terms[:, 0, :]
    row_count = head_rows.shape[1]
    width = inputs.shape[2]
    slot_count = param_slots.shape[1]
    pair_most = slot_count // dp_count
    block_rows = row_count // dp_count
    split_at = (PROJ - 1) * DKV
    first_part = jnp.einsum(
        "tr,td->rd", head_rows[:, :split_at], inputs[:, 0, :], preferred_element_type=jnp.float32
    )
    last_part = jnp.einsum(
        "tr,td->rd", head_rows[:, split_at:], inputs[:, 1, :], preferred_element_type=jnp.float32
    )
    gradient = jnp.concatenate([first_part, last_part], axis=0)
    slot_row, live_mask = slot_table(owner_list[0, :, 0], dp_count, pair_most)
    home_sum = lax.psum_scatter(gradient, "dp", scatter_dimension=0, tiled=True)
    local_rows = (
        lax.dynamic_slice_in_dim(slot_row, my_index * pair_most, pair_most, 1)
        - my_index * block_rows
    )
    outgoing = jnp.take(home_sum, local_rows.reshape(-1), axis=0, mode="clip").reshape(
        dp_count, pair_most, width
    )
    received = lax.all_to_all(outgoing, "dp", split_axis=0, concat_axis=0, tiled=True)
    slot_grad = received.reshape(slot_count, width)
    my_rows = lax.dynamic_index_in_dim(slot_row, my_index, 0, keepdims=False)
    live_f = lax.dynamic_index_in_dim(live_mask, my_index, 0, keepdims=False).astype(jnp.float32)
    grad_sq = slot_grad * slot_grad + EPS_SQUARE
    row_val = DECAY_RATE * row_state[0] + (1.0 - DECAY_RATE) * jnp.mean(grad_sq, axis=1)
    slot_pick = ((my_rows // DKV)[:, None] == jnp.arange(PROJ, dtype=jnp.int32)[None, :]).astype(
        jnp.float32
    )
    live_pick = slot_pick * live_f[:, None]
    col_part = jnp.einsum("sp,sd->pd", live_pick, grad_sq, precision=lax.Precision.HIGHEST)
    row_part = jnp.sum(live_pick * row_val[:, None], axis=0)
    col_sum, row_total = lax.psum((col_part, row_part), "dp")
    new_col = DECAY_RATE * col_state[0] + (1.0 - DECAY_RATE) * col_sum / DKV
    row_mean = row_total / DKV
    col_at = jnp.dot(slot_pick, new_col, precision=lax.Precision.HIGHEST)
    mean_at = jnp.sum(slot_pick * row_mean[None, :], axis=1)
    second_moment = row_val[:, None] * col_at / mean_at[:, None]
    update = slot_grad / jnp.sqrt(second_moment)
    new_param = (
        (param_slots[0].astype(jnp.float32) - STEP_SIZE * update) * live_f[:, None]
    ).astype(jnp.bfloat16)
    return (new_param[None], (row_val * live_f)[None], new_col[None])


def solution(mesh):
    placed = (
        P("dp", "shard", None),
        P("dp", None, None),
        P("shard", None, None),
        P("shard", "dp", None),
        P("shard", "dp"),
        P("shard", None, None),
    )
    return jax.shard_map(
        on_device,
        mesh=mesh,
        in_specs=placed,
        out_specs=(P("shard", "dp", None), P("shard", "dp"), P("shard", None, None)),
        check_vma=False,
    )
```

profile of v0, /device:TPU:1, one launch (start us, length us, event | category | flops | bytes accessed | tf_op | source)
XLA Modules:
  0.0 534.9 jit_solution(12168879802513031729)
XLA Ops:
  7.2 0.0 copy-start
  7.2 0.0 reduce-scatter.2.cloned.1.call-start
  7.2 6.2 %fusion.32 = (bf16[128,1,4096]{2,1,0:T(2,128)(2,1)S(1)}, bf16[128,1,4096]{2,1,0:T(2,128)(2,1)S(1)}) fusion(bf16[128,2,4096]{2,1,0:T(2,128)(2,1)} %param.7), kind=kLoop, calls=%fused_computation.66 | loop fusion | bytes 4194304 | tf_op jit(solution)/shard_map/slice | solution.py:48
  13.4 0.0 copy-done
  13.4 1.3 fusion.9
  14.7 1.5 fusion.10
  16.2 2.2 pad_maximum_fusion
  18.4 0.0 copy-start.2
  18.5 0.0 reduce-scatter.2.cloned.1.call-update
  18.5 0.5 broadcast.208
  19.0 0.1 copy-done.2
  19.1 0.7 reduce.10
  19.8 0.1 eq.94
  19.9 0.1 copy.41
  19.9 0.5 fusion.33
  20.4 0.1 copy.42
  20.5 0.1 eq.98
  20.7 1.2 fusion.12
  21.9 0.1 copy.43
  22.0 0.1 copy.44
  22.1 0.1 reshape.203
  22.2 245.5 %reduce-scatter.2.cloned.1.call-done = f32[16,4096]{1,0:T(8,128)} async-done(((f32[256,4096]{1,0:T(8,128)}), f32[16,4096]{1,0:T(8,128)}) %reduce-scatter.2.cloned.1.call-update) | async-done | bytes 262160 | tf_op jit(solution)/shard_map/reduce_scatter | solution.py:55
  267.7 1.9 gather_fusion
  269.6 0.0 copy-start.3
  269.6 0.0 copy-start.1
  269.6 1.1 reshape.197
  270.7 0.0 copy-start.4
  270.7 5.1 all-to-all-start
  275.8 0.0 all-reduce.2.cloned.1.call-start
  275.9 0.0 copy-done.3
  275.9 0.1 copy.45
  276.0 0.1 copy.46
  276.1 0.2 dynamic-slice_reduce_fusion
  276.3 12.9 %all-to-all-done = f32[16,2,4096]{2,1,0:T(2,128)S(1)} async-done(((f32[16,2,4096]{2,1,0:T(2,128)}), f32[16,2,4096]{2,1,0:T(2,128)S(1)}, u32[]{:S(2)}, u32[]{:S(2)}) %all-to-all-start) | async-done | bytes 524320 | tf_op jit(solution)/shard_map/all_to_all | solution.py:63
  289.2 0.4 add_reduce_fusion
  289.6 0.1 mul.141
  289.6 0.1 mul.123
  289.7 0.2 add_multiply_fusion
  289.9 0.1 fusion.23
  290.0 42.6 %psum.15 = f32[4]{0:T(128)S(1)} all-reduce(f32[4]{0:T(128)S(1)} %fusion.23), channel_id=1, replica_groups=mesh['dp'=16,'shard'=64] {'dp'}, use_global_device_ids=true, to_apply=%region_8.9 | all-reduce | flops 4 | bytes 32 | tf_op jit(solution)/shard_map/psum | solution.py:75
  332.7 0.4 reshape.198
  333.1 1.0 fusion.13
  334.1 0.0 all-reduce.2.cloned.1.call-update
  334.1 0.6 copy.48
  334.7 0.1 select_reduce_fusion
  334.8 189.7 %all-reduce.2.cloned.1.call-done = f32[4,4096]{1,0:T(4,128)} async-done(((f32[4,4096]{1,0:T(4,128)}), f32[4,4096]{1,0:T(4,128)}) %all-reduce.2.cloned.1.call-update) | async-done | bytes 65552 | tf_op jit(solution)/shard_map/psum | solution.py:75
  524.5 0.0 copy-done.1
  524.5 1.5 fusion.21
  526.0 0.0 copy-done.4
  526.0 2.1 fusion.7
  (10 shorter events, 0.1 us)
Async XLA Ops:
  7.2 6.2 %copy-start = (bf16[128,1,256]{2,0,1:T(8,128)(2,1)S(1)}, bf16[128,1,256]{2,0,1:T(8,128)(2,1)}, u32[]{:S(2)}) copy-start(bf16[128,1,256]{2,0,1:T(8,128)(2,1)} %param.6) | copy-start | bytes 196612
  7.2 260.5 %reduce-scatter.2.cloned.1.call-start = ((), (), s32[]{:S(2)}) async-start(), calls=%async_computation.2 | async-start | bytes 4456448 | tf_op jit(solution)/shard_map/reduce_scatter | solution.py:55
  18.4 0.7 copy-start.2
  269.6 6.3 %copy-start.3 = (f32[1,32]{1,0:T(1,128)S(1)}, f32[1,32]{1,0:T(1,128)}, u32[]{:S(2)}) copy-start(f32[1,32]{1,0:T(1,128)} %param.10) | copy-start | bytes 388
  269.6 254.9 %copy-start.1 = (f32[1,4,4096]{2,1,0:T(4,128)S(1)}, f32[1,4,4096]{2,1,0:T(4,128)}, u32[]{:S(2)}) copy-start(f32[1,4,4096]{2,1,0:T(4,128)} %param.11) | copy-start | bytes 196612
  270.7 255.3 %copy-start.4 = (bf16[1,32,4096]{2,1,0:T(8,128)(2,1)S(1)}, bf16[1,32,4096]{2,1,0:T(8,128)(2,1)}, u32[]{:S(2)}) copy-start(bf16[1,32,4096]{2,1,0:T(8,128)(2,1)} %param.9) | copy-start | bytes 786436
  270.7 18.5 %all-to-all-start = ((f32[16,2,4096]{2,1,0:T(2,128)}), f32[16,2,4096]{2,1,0:T(2,128)S(1)}, u32[]{:S(2)}, u32[]{:S(2)}) async-start(f32[16,2,4096]{2,1,0:T(2,128)} %reshape.197), calls=%async_computation.1 | async-start | bytes 1048576 | tf_op jit(solution)/shard_map/all_to_all | solution.py:63
  275.8 248.7 %all-reduce.2.cloned.1.call-start = ((), (), s32[]{:S(2)}) async-start(), calls=%async_computation.3 | async-start | bytes 131072 | tf_op jit(solution)/shard_map/psum | solution.py:75
Sparse Core Ops, SparseCore 0:
  18.6 249.0 reduce-scatter.1
  334.2 190.2 all-reduce.1
where the time goes:
time: 542 us; the launch traced here: 535 us
  waiting for transfers between devices  448 us (83%)
  blocking collectives  42.6 us (8%)
  between operations  14.2 us (3%)
  local copies, waits for them, and re-layouts  11.9 us (2%)
  other arithmetic  6.9 us (1%)
  matrix products  5.91 us (1%)
    reduce_scatter x1, waiting for transfers between devices, on_device(): home_sum = lax.psum_scatter(gradient, 'dp', scatter_dimension=0, tiled=True)  246 us
    psum x1, waiting for transfers between devices, on_device(): col_sum, row_total = lax.psum((col_part, row_part), 'dp')  190 us
    psum x1, blocking collectives, on_device(): col_sum, row_total = lax.psum((col_part, row_part), 'dp')  42.6 us
    all_to_all x1, waiting for transfers between devices, on_device(): lax.all_to_all(outgoing, 'dp', split_axis=0, concat_axis=0, tiled=True)  12.9 us
  transfers between devices with their start and end apart: 3, of which 3 were waited for; matrix products, arithmetic and copies ran while one was open for 1% of the time, Pallas kernels for 0%

commit v1 on v0

v1 whole, which is shorter than its diff:
```python
import jax
import jax.numpy as jnp
from jax import lax
from jax.experimental import pallas as pl
from jax.experimental.pallas import tpu as pltpu
from jax.sharding import PartitionSpec as P

MESH = pl.DeviceIdType.MESH
EPS_SQUARE = 1e-30
F32 = jnp.float32
BF16 = jnp.bfloat16
NT = (((1,), (1,)), ((), ()))


def place():
    dp = lax.axis_index("dp")
    shard = lax.axis_index("shard")
    return dp, dp // 8, dp % 8, shard, shard // 16, (shard // 2) % 8, shard % 2


def kernel(hf, ip, own_row, own_col, rs_col, params, cols,
           out_p, out_r, out_c,
           hb, ib, hst, acc, gs, rb, sown, sb, pbuf, cbuf,
           ssh, rsh, ssi, rsi, ssy, rsy, ssc, rsc, sss, rss, ssg, rsg, loc):
    dp, a, z, shard, xl, y, c = place()
    other = 1 - a
    far_shard = (3 - xl) * 16 + y * 2 + c
    mate = xl * 16 + y * 2 + 1 - c
    fwd = lax.rem(y + 1 - 2 * c + 8, 8)
    back = lax.rem(y - 1 + 2 * c + 8, 8)
    fwd_shard = xl * 16 + fwd * 2 + c
    back_shard = xl * 16 + back * 2 + c
    right = (a * 8 + lax.rem(z + 1, 8), shard)
    left = (a * 8 + lax.rem(z + 7, 8), shard)

    def near(n):
        return a * 8 + lax.rem(z + n, 8)

    def far(n):
        return other * 8 + lax.rem(z + n, 8)

    peers = [near(n) for n in range(1, 8)] + [far(n) for n in range(8)]

    barrier = pltpu.get_barrier_semaphore()
    greeted = [(d, shard) for d in peers] + [(far(n), far_shard) for n in range(8)]
    greeted += [(dp, mate), (dp, fwd_shard), (dp, back_shard)]
    for who in greeted:
        pl.semaphore_signal(barrier, inc=1, device_id=who, device_id_type=MESH)

    local = [
        pltpu.make_async_copy(hf, hb.at[dp], loc.at[0]),
        pltpu.make_async_copy(ip.at[dp], ib.at[c, y, dp], loc.at[1]),
        pltpu.make_async_copy(params, pbuf, loc.at[2]),
        pltpu.make_async_copy(cols, cbuf, loc.at[3]),
    ]
    for cp in local:
        cp.start()

    pl.semaphore_wait(barrier, len(greeted))

    sent = []

    def send(src, dst, s_sem, r_sem, who):
        cp = pltpu.make_async_remote_copy(
            src_ref=src, dst_ref=dst, send_sem=s_sem, recv_sem=r_sem, device_id=who, device_id_type=MESH
        )
        cp.start()
        sent.append(cp)

    def arrived(ref, sem):
        pltpu.make_async_copy(ref, ref, sem).wait()

    count = [0]

    def send_h(d, who, src=None):
        send(hb.at[d] if src is None else src, hb.at[d], ssh.at[count[0]], rsh.at[d], who)
        count[0] += 1

    for i, n in enumerate((4, 3, 5, 2, 6, 1, 7, 0)):
        d = far(n)
        send(ip.at[d], ib.at[c, y, dp], ssi.at[i], rsi.at[dp], (d, far_shard))
    for i, n in enumerate((4, 3, 5, 2, 6, 1, 7)):
        d = near(n)
        send(ip.at[d], ib.at[c, y, dp], ssi.at[8 + i], rsi.at[dp], (d, shard))
    send_h(dp, (far(0), shard), hf)
    send_h(dp, right, hf)
    send_h(dp, left, hf)

    row_id = lax.broadcasted_iota(jnp.int32, (256, 256), 0)
    lane_id = lax.broadcasted_iota(jnp.int32, (256, 256), 1)
    owner = own_row[...]
    before = (own_col[...] == owner) & ((row_id >> 4) == (lane_id >> 4)) & (row_id < lane_id)
    rank = jnp.sum(before.astype(F32), axis=0, keepdims=True).astype(jnp.int32)
    rows = lax.broadcasted_iota(jnp.int32, (1, 256), 1)
    key = owner * 32 + (rows >> 4) * 2 + rank
    k0 = lax.broadcasted_iota(jnp.int32, (16, 24, 1), 0) * 32 + lax.broadcasted_iota(jnp.int32, (16, 24, 1), 1)
    k1 = lax.broadcasted_iota(jnp.int32, (16, 8, 1), 0) * 32 + 24 + lax.broadcasted_iota(jnp.int32, (16, 8, 1), 1)
    pick0 = (k0.reshape(384, 1) == key).astype(F32).astype(BF16)
    pick1 = (k1.reshape(128, 1) == key).astype(F32).astype(BF16)
    mine = lax.broadcasted_iota(jnp.int32, (32, 256), 0) + dp * 32
    live = jnp.sum((mine == key).astype(F32), axis=1, keepdims=True)
    slot8 = lax.broadcasted_iota(jnp.int32, (32, 128), 0) >> 3
    lane = lax.broadcasted_iota(jnp.int32, (32, 128), 1)
    sown[...] = jnp.sum(jnp.where(slot8 == (lane >> 5), live * rs_col[...], 0.0), axis=0, keepdims=True)
    for i, d in enumerate(peers):
        send(sown, sb.at[dp], sss.at[i], rss.at[dp], (d, shard))

    def got_h(d):
        arrived(hb.at[d], rsh.at[d])

    def send_y(yy, i, who):
        send(ib.at[c, yy], ib.at[c, yy], ssy.at[i], rsy.at[yy], (dp, who))

    def send_c(yy, i):
        send(ib.at[c, yy], ib.at[c, yy], ssc.at[i], rsc.at[yy], (dp, mate))

    def upstream(n):
        return lax.rem(y - n + 2 * n * c + 8, 8)

    def downstream(n):
        return lax.rem(y + n - 2 * n * c + 8, 8)

    def h_own(s):
        d = near(8 - s)
        got_h(d)
        if s < 4:
            send_h(d, right)
        if s < 4:
            d = near(s)
            got_h(d)
            if s < 3:
                send_h(d, left)

    def h_far(s):
        if s == 0:
            got_h(far(0))
            send_h(far(0), right)
            send_h(far(0), left)
            return
        if s < 4:
            d = far(8 - s)
            got_h(d)
            if s < 3:
                send_h(d, right)
        d = far(s)
        got_h(d)
        if s < 4:
            send_h(d, left)

    def i_ring(s):
        if s == 0:
            local[1].wait()
            for d in peers:
                arrived(ib.at[c, y, d], rsi.at[d])
            send_y(y, 0, fwd_shard)
            send_y(y, 1, back_shard)
            send_c(y, 0)
            return
        yy = upstream(s)
        arrived(ib.at[c, yy], rsy.at[yy])
        if s < 4:
            send_y(yy, 2 * s, fwd_shard)
        send_c(yy, 2 * s)
        if s < 4:
            yy = downstream(s)
            arrived(ib.at[c, yy], rsy.at[yy])
            if s < 3:
                send_y(yy, 2 * s + 1, back_shard)
            send_c(yy, 2 * s - 1)

    h_own(1)
    i_ring(0)
    h_far(0)
    h_own(2)
    h_far(1)
    i_ring(1)
    h_own(3)
    h_far(2)
    i_ring(2)
    h_own(4)
    h_far(3)
    i_ring(3)
    h_far(4)
    local[0].wait()

    for yy in range(8):
        h = hb[:, yy * 16:(yy + 1) * 16, :].reshape(256, 256).astype(BF16)
        hst[yy, 0:384, :] = lax.dot_general(pick0, h, NT, preferred_element_type=F32).astype(BF16)
        hst[yy, 384:512, :] = lax.dot_general(pick1, h, NT, preferred_element_type=F32).astype(BF16)

    i_ring(4)
    for n in range(8):
        yy = lax.rem(y + n, 8)
        arrived(ib.at[1 - c, yy], rsc.at[yy])

    acc[...] = jnp.zeros_like(acc)

    def tokens(yy, carry):
        w0 = ib[0, yy].reshape(256, 256).astype(BF16)
        w1 = ib[1, yy].reshape(256, 256).astype(BF16)
        acc[0:384, :] += jnp.dot(hst[yy, 0:384, :], w0, preferred_element_type=F32)
        acc[384:512, :] += jnp.dot(hst[yy, 384:512, :], w1, preferred_element_type=F32)
        return carry

    lax.fori_loop(0, 8, tokens, 0)

    for half in range(2):
        g0 = acc[0:384, half * 128:(half + 1) * 128].reshape(16, 24, 128)
        g1 = acc[384:512, half * 128:(half + 1) * 128].reshape(16, 8, 128)
        gs[:, half * 32:half * 32 + 24, :] = g0
        gs[:, half * 32 + 24:half * 32 + 32, :] = g1
        q0 = jnp.sum(jnp.sum((g0 * g0).reshape(16, 3, 8, 128), axis=0), axis=1)
        q1 = jnp.sum(jnp.sum(g1 * g1, axis=0), axis=0, keepdims=True)
        q = jnp.concatenate([q0, q1], axis=0)
        gs[:, 64 + half * 4:68 + half * 4, :] = jnp.broadcast_to(q[None], (16, 4, 128))

    for i, n in enumerate((4, 3, 5, 2, 6, 1, 7, 0)):
        d = far(n)
        send(gs.at[d], rb.at[dp], ssg.at[i], rsg.at[dp], (d, shard))
    for i, n in enumerate((4, 3, 5, 2, 6, 1, 7)):
        d = near(n)
        send(gs.at[d], rb.at[dp], ssg.at[8 + i], rsg.at[dp], (d, shard))
    keep = pltpu.make_async_copy(gs.at[dp], rb.at[dp], loc.at[4])
    keep.start()
    keep_s = pltpu.make_async_copy(sown, sb.at[dp], loc.at[5])
    keep_s.start()
    keep.wait()
    keep_s.wait()
    local[2].wait()
    local[3].wait()
    for d in peers:
        arrived(sb.at[d], rss.at[d])
    for d in peers:
        arrived(rb.at[d], rsg.at[d])

    sq = jnp.zeros((32, 128), F32)
    cs = jnp.zeros((4, 128), F32)
    for d in range(16):
        for half in range(2):
            g = rb[d, half * 32:half * 32 + 32, :]
            sq = sq + g * g
            cs = cs + rb[d, 64 + half * 4:68 + half * 4, :]
    row_val = 0.5 * rs_col[...] + 0.5 * (jnp.sum(sq, axis=1, keepdims=True) / 4096.0 + EPS_SQUARE)
    cs = cs + 64.0 * 32.0 * EPS_SQUARE
    all_cs = jnp.sum(jnp.broadcast_to(cs[:, None, :], (4, 8, 128)).reshape(32, 128), axis=1, keepdims=True)
    states = jnp.sum(sb[...], axis=0)
    all_st = jnp.sum(jnp.where(lane == slot8 * 32, states, 0.0), axis=1, keepdims=True)
    row_mean = (0.5 * all_st + 0.5 * (all_cs / 4096.0)) / 64.0
    by_row = 0.5 * lax.rsqrt(row_val / row_mean)
    out_r[...] = row_val * live
    for d in range(16):
        for half in range(2):
            at = d * 256 + half * 128
            q = rb[d, 64 + half * 4:68 + half * 4, :]
            new_col = 0.5 * cbuf[:, at:at + 128] + 0.5 * (q + 64.0 * EPS_SQUARE) / 64.0
            out_c[:, at:at + 128] = new_col
            by_col = jnp.broadcast_to(lax.rsqrt(new_col)[:, None, :], (4, 8, 128)).reshape(32, 128)
            g = rb[d, half * 32:half * 32 + 32, :]
            par = pbuf[:, at:at + 128].astype(F32)
            out_p[:, at:at + 128] = ((par - g * by_row * by_col) * live).astype(BF16)

    for cp in sent:
        cp.wait_send()


def on_device(head_terms, inputs, owner_list, param_slots, row_state, col_state):
    dp, a, z, shard, xl, y, c = place()
    hf = head_terms[:, 0, :].astype(F32)
    piece = lax.dynamic_slice(inputs, (16 * y, c, 0), (16, 1, 4096)).reshape(16, 16, 256)
    ip = jnp.transpose(piece, (1, 0, 2)).astype(F32)
    vm = pl.BlockSpec(memory_space=pltpu.VMEM)
    hbm = pl.BlockSpec(memory_space=pl.ANY)
    dma = pltpu.SemaphoreType.DMA
    new_params, new_rows, new_cols = pl.pallas_call(
        kernel,
        out_shape=(
            jax.ShapeDtypeStruct((32, 4096), BF16),
            jax.ShapeDtypeStruct((32, 1), F32),
            jax.ShapeDtypeStruct((4, 4096), F32),
        ),
        in_specs=[hbm, hbm, vm, vm, vm, hbm, hbm],
        out_specs=(vm, vm, vm),
        scratch_shapes=[
            pltpu.VMEM((16, 128, 256), F32),
            pltpu.VMEM((2, 8, 16, 16, 256), F32),
            pltpu.VMEM((8, 512, 256), BF16),
            pltpu.VMEM((512, 256), F32),
            pltpu.VMEM((16, 72, 128), F32),
            pltpu.VMEM((16, 72, 128), F32),
            pltpu.VMEM((1, 128), F32),
            pltpu.VMEM((16, 1, 128), F32),
            pltpu.VMEM((32, 4096), BF16),
            pltpu.VMEM((4, 4096), F32),
            dma((15,)), dma((16,)),
            dma((15,)), dma((16,)),
            dma((7,)), dma((8,)),
            dma((9,)), dma((8,)),
            dma((15,)), dma((16,)),
            dma((15,)), dma((16,)),
            dma((6,)),
        ],
        compiler_params=pltpu.CompilerParams(collective_id=0, has_side_effects=True, vmem_limit_bytes=40 << 20),
    )(
        hf,
        ip,
        owner_list.reshape(1, 256),
        owner_list.reshape(256, 1),
        row_state.reshape(32, 1),
        param_slots.reshape(32, 4096),
        col_state.reshape(4, 4096),
    )
    return (new_params[None], new_rows.reshape(1, 32), new_cols[None])


def solution(mesh):
    placed = (
        P("dp", "shard", None),
        P("dp", None, None),
        P("shard", None, None),
        P("shard", "dp", None),
        P("shard", "dp"),
        P("shard", None, None),
    )
    return jax.shard_map(
        on_device,
        mesh=mesh,
        in_specs=placed,
        out_specs=(P("shard", "dp", None), P("shard", "dp"), P("shard", None, None)),
        check_vma=False,
    )
```

time: 542 us -> 95 us (0.18); the launches traced: 535 us -> 93.8 us
  waiting for transfers between devices: 448 us -> 0 us
  Pallas kernels: 0 us -> 84.5 us
  blocking collectives: 42.6 us -> 0 us
  between operations: 14.2 us -> 0.72 us
  local copies, waits for them, and re-layouts: 11.9 us -> 5.36 us
  matrix products: 5.91 us -> 0 us
    reduce_scatter x1 -> x0, waiting for transfers between devices: 246 us -> none  [on_device(): home_sum = lax.psum_scatter(gradient, 'dp', scatter_dimension=0, tiled=True)]
    psum x1 -> x0, waiting for transfers between devices: 190 us -> none  [on_device(): col_sum, row_total = lax.psum((col_part, row_part), 'dp')]
    pallas_call x0 -> x1, Pallas kernels: none -> 84.5 us  [on_device(): pl.pallas_call(kernel, out_shape=(jax.ShapeDtypeStruct((32, 4096), BF16),...]
    psum x1 -> x0, blocking collectives: 42.6 us -> none  [on_device(): col_sum, row_total = lax.psum((col_part, row_part), 'dp')]
    all_to_all x1 -> x0, waiting for transfers between devices: 12.9 us -> none  [on_device(): lax.all_to_all(outgoing, 'dp', split_axis=0, concat_axis=0, tiled=True)]
    slice x1 -> x0, local copies, waits for them, and re-layouts: 6.18 us -> none  [on_device(): inputs[:, 0, :]]
    dot_general x4 -> x0, matrix products: 5.91 us -> none  [the longest x1 2.07 us: on_device(): col_at = jnp.dot(slot_pick, new_col, precision=lax.Precision.HIGHEST)]
  transfers between devices with their start and end apart: 3 -> 0, of which waited for: 3 -> 0; matrix products, arithmetic and copies ran while one was open for 1% -> 0% of each run, Pallas kernels for 0% -> 0%
where the time goes in v1:
time: 95 us; the launch traced here: 93.8 us
  Pallas kernels  84.5 us (89%)
  local copies, waits for them, and re-layouts  5.36 us (6%)
  other arithmetic  3.2 us (3%)
    pallas_call x1, Pallas kernels, on_device(): pl.pallas_call(kernel, out_shape=(jax.ShapeDtypeStruct((32, 4096), BF16),...  84.5 us
    unnamed x8, local copies, waits for them, and re-layouts  3.79 us

profile of v1, /device:TPU:1, one launch (start us, length us, event | category | flops | bytes accessed | tf_op | source)
XLA Modules:
  0.0 93.8 jit_solution(6026952525760847426)
XLA Ops:
  0.7 0.7 copy.12.rs_col
  1.4 0.8 bitcast_convert_fusion.hf
  2.3 0.8 copy.11.own_col
  3.1 1.7 %convert_reduce_fusion = f32[16,4096]{1,0:T(8,128)S(1)} fusion(bf16[128,2,4096]{2,1,0:T(2,128)(2,1)} %param.7, s32[]{:T(128)S(6)} %select_n.23, s32[]{:T(128)S(6)} %select_n.25), kind=kLoop, calls=%fused_computation.1 | loop fusion | flops 65536 | bytes 393224 | tf_op jit(solution)/shard_map/convert_element_type | solution.py:270
  4.8 0.0 copy-start
  4.8 0.9 %copy-done = bf16[1,32,4096]{2,1,0:T(8,128)(2,1)S(1)} copy-done((bf16[1,32,4096]{2,1,0:T(8,128)(2,1)S(1)}, bf16[1,32,4096]{2,1,0:T(8,128)(2,1)}, u32[]{:S(2)}) %copy-start) | copy-done | bytes 262168
  5.8 0.0 copy-start.1
  5.8 0.8 copy-done.1
  6.6 0.0 copy-start.2
  6.6 0.7 copy-done.2
  7.3 84.5 %shard_map.85 = (bf16[32,4096]{1,0:T(8,128)(2,1)S(1)}, f32[32,1]{1,0:T(8,128)S(1)}, f32[4,4096]{1,0:T(4,128)S(1)}) custom-call(f32[128,256]{1,0:T(8,128)S(1)} %bitcast_convert_fusion.hf, f32[16,16,256]{2,1,0:T(8,128)S(1)} %bitcast.18, s32[1,256]{1,0:T(1,128)S(1)} %bitcast.24, s32[256,1]{1,0:T(8,128)S(1)} %copy.11.own_col, f32[32,1]{1,0:T(8,128)S(1)} %copy.12.rs_col, ...), custom_call_target="tpu_custom_call" | custom-call | tf_op jit(solution)/shard_map/pallas_call | solution.py:274
  91.8 0.6 reduce.1
  92.5 0.7 copy.18
  93.2 0.6 copy.19
  (1 shorter events, 0.0 us)
Async XLA Ops:
  4.8 1.0 %copy-start = (bf16[1,32,4096]{2,1,0:T(8,128)(2,1)S(1)}, bf16[1,32,4096]{2,1,0:T(8,128)(2,1)}, u32[]{:S(2)}) copy-start(bf16[1,32,4096]{2,1,0:T(8,128)(2,1)} %param.9) | copy-start | bytes 786436
  5.8 0.8 copy-start.1
  6.6 0.7 copy-start.2

commit v2 on v1

v2 whole, which is shorter than its diff:
```python
import jax
import jax.numpy as jnp
from jax import lax
from jax.experimental import pallas as pl
from jax.experimental.pallas import tpu as pltpu
from jax.sharding import PartitionSpec as P

MESH = pl.DeviceIdType.MESH
EPS_SQUARE = 1e-30
F32 = jnp.float32
BF16 = jnp.bfloat16
NT = (((1,), (1,)), ((), ()))


def place():
    dp = lax.axis_index("dp")
    shard = lax.axis_index("shard")
    return dp, dp // 8, dp % 8, shard, shard // 16, (shard // 2) % 8, shard % 2


def row_keys(owner):
    row_id = lax.broadcasted_iota(jnp.int32, (256, 256), 0)
    lane_id = lax.broadcasted_iota(jnp.int32, (256, 256), 1)
    same = (row_id == lane_id).astype(F32)
    own_col = jnp.sum(same * owner.astype(F32), axis=1, keepdims=True).astype(jnp.int32)
    before = (own_col == owner) & ((row_id >> 4) == (lane_id >> 4)) & (row_id < lane_id)
    rank = jnp.sum(before.astype(F32), axis=0, keepdims=True).astype(jnp.int32)
    rows = lax.broadcasted_iota(jnp.int32, (1, 256), 1)
    return owner * 32 + (rows >> 4) * 2 + rank


def own_slots(key, dp, states):
    mine = lax.broadcasted_iota(jnp.int32, (32, 256), 0) + dp * 32
    live = jnp.sum((mine == key).astype(F32), axis=1, keepdims=True)
    eye = lax.broadcasted_iota(jnp.int32, (32, 32), 0) == lax.broadcasted_iota(jnp.int32, (32, 32), 1)
    row_st = jnp.sum(jnp.where(eye, states, 0.0), axis=1, keepdims=True)
    return live, row_st, eye


def exchange(heads, inputs, owners, states, rb, sb,
             hraw, iraw, ipf, hb, ib, hst, acc, gs, sown,
             ssh, rsh, ssi, rsi, ssy, rsy, ssc, rsc, sss, rss, ssg, rsg, loc):
    dp, a, z, shard, xl, y, c = place()
    other = 1 - a
    far_shard = (3 - xl) * 16 + y * 2 + c
    mate = xl * 16 + y * 2 + 1 - c
    fwd = lax.rem(y + 1 - 2 * c + 8, 8)
    back = lax.rem(y - 1 + 2 * c + 8, 8)
    fwd_shard = xl * 16 + fwd * 2 + c
    back_shard = xl * 16 + back * 2 + c
    right = (a * 8 + lax.rem(z + 1, 8), shard)
    left = (a * 8 + lax.rem(z + 7, 8), shard)

    def near(n):
        return a * 8 + lax.rem(z + n, 8)

    def far(n):
        return other * 8 + lax.rem(z + n, 8)

    peers = [near(n) for n in range(1, 8)] + [far(n) for n in range(8)]

    barrier = pltpu.get_barrier_semaphore()
    greeted = [(d, shard) for d in peers] + [(far(n), far_shard) for n in range(8)]
    greeted += [(dp, mate), (dp, fwd_shard), (dp, back_shard)]
    for who in greeted:
        pl.semaphore_signal(barrier, inc=1, device_id=who, device_id_type=MESH)

    local = [
        pltpu.make_async_copy(inputs.at[pl.ds(16 * y, 16)], iraw, loc.at[0]),
        pltpu.make_async_copy(heads, hraw, loc.at[1]),
    ]
    for cp in local:
        cp.start()

    local[0].wait()
    which = lax.broadcasted_iota(jnp.int32, (16, 2, 256), 1) == c

    for d in range(16):
        pair = iraw[:, :, d * 256:(d + 1) * 256].astype(F32)
        ipf[d] = jnp.sum(jnp.where(which, pair, 0.0), axis=1)
    ib[c, y, dp] = ipf[dp]
    local[1].wait()
    hb[dp] = hraw[...].astype(F32)
    pl.semaphore_wait(barrier, len(greeted))

    sent = []

    def send(src, dst, s_sem, r_sem, who):
        cp = pltpu.make_async_remote_copy(
            src_ref=src, dst_ref=dst, send_sem=s_sem, recv_sem=r_sem, device_id=who, device_id_type=MESH
        )
        cp.start()
        sent.append(cp)

    def arrived(ref, sem):
        pltpu.make_async_copy(ref, ref, sem).wait()

    count = [0]

    def send_h(d, who):
        send(hb.at[d], hb.at[d], ssh.at[count[0]], rsh.at[d], who)
        count[0] += 1

    for i, n in enumerate((4, 3, 5, 2, 6, 1, 7, 0)):
        d = far(n)
        send(ipf.at[d], ib.at[c, y, dp], ssi.at[7 + i], rsi.at[dp], (d, far_shard))
    for i, n in enumerate((4, 3, 5, 2, 6, 1, 7)):
        d = near(n)
        send(ipf.at[d], ib.at[c, y, dp], ssi.at[i], rsi.at[dp], (d, shard))
    send_h(dp, (far(0), shard))
    send_h(dp, right)
    send_h(dp, left)

    key = row_keys(owners[...])
    k0 = lax.broadcasted_iota(jnp.int32, (16, 24, 1), 0) * 32 + lax.broadcasted_iota(jnp.int32, (16, 24, 1), 1)
    k1 = lax.broadcasted_iota(jnp.int32, (16, 8, 1), 0) * 32 + 24 + lax.broadcasted_iota(jnp.int32, (16, 8, 1), 1)
    pick0 = (k0.reshape(384, 1) == key).astype(F32).astype(BF16)
    pick1 = (k1.reshape(128, 1) == key).astype(F32).astype(BF16)
    live, row_st, _ = own_slots(key, dp, states[...])
    slot8 = lax.broadcasted_iota(jnp.int32, (32, 128), 0) >> 3
    lane = lax.broadcasted_iota(jnp.int32, (32, 128), 1)
    sown[...] = jnp.sum(jnp.where(slot8 == (lane >> 5), live * row_st, 0.0), axis=0, keepdims=True)
    for i, d in enumerate(peers):
        send(sown, sb.at[dp], sss.at[i], rss.at[dp], (d, shard))

    def got_h(d):
        arrived(hb.at[d], rsh.at[d])

    quads = (dp // 4, a * 2 + 1 - z // 4, other * 2 + z // 4, other * 2 + 1 - z // 4)

    def chunk(core, yy, g):
        return ib.at[core, yy, pl.ds(4 * quads[g], 4)]

    def send_y(yy, g, i, who):
        send(chunk(c, yy, g), chunk(c, yy, g), ssy.at[i, g], rsy.at[yy, g], (dp, who))

    def send_c(yy, g, i):
        send(chunk(c, yy, g), chunk(c, yy, g), ssc.at[i, g], rsc.at[yy, g], (dp, mate))

    def upstream(n):
        return lax.rem(y - n + 2 * n * c + 8, 8)

    def downstream(n):
        return lax.rem(y + n - 2 * n * c + 8, 8)

    def h_own(s):
        d = near(8 - s)
        got_h(d)
        if s < 4:
            send_h(d, right)
        if s < 4:
            d = near(s)
            got_h(d)
            if s < 3:
                send_h(d, left)

    def h_far(s):
        if s == 0:
            got_h(far(0))
            send_h(far(0), right)
            send_h(far(0), left)
            return
        if s < 4:
            d = far(8 - s)
            got_h(d)
            if s < 3:
                send_h(d, right)
        d = far(s)
        got_h(d)
        if s < 4:
            send_h(d, left)

    def i_ring(s, *groups):
        for g in groups:
            if s == 0:
                if g == 0:
                    for k in range(1, 4):
                        d = dp - z % 4 + lax.rem(z + k, 4)
                        arrived(ib.at[c, y, d], rsi.at[d])
                else:
                    for k in range(4):
                        d = 4 * quads[g] + k
                        arrived(ib.at[c, y, d], rsi.at[d])
                send_y(y, g, 0, fwd_shard)
                send_y(y, g, 1, back_shard)
                send_c(y, g, 0)
                continue
            yy = upstream(s)
            arrived(chunk(c, yy, g), rsy.at[yy, g])
            if s < 4:
                send_y(yy, g, 2 * s, fwd_shard)
            send_c(yy, g, 2 * s - 1)
            if s < 4:
                yy = downstream(s)
                arrived(chunk(c, yy, g), rsy.at[yy, g])
                if s < 3:
                    send_y(yy, g, 2 * s + 1, back_shard)
                send_c(yy, g, 2 * s)

    h_own(1)
    i_ring(0, 0, 1)
    h_far(0)
    h_own(2)
    i_ring(0, 2, 3)
    i_ring(1, 0, 1)
    h_far(1)
    i_ring(1, 2, 3)
    h_own(3)
    i_ring(2, 0, 1)
    h_far(2)
    i_ring(2, 2, 3)
    h_own(4)
    i_ring(3, 0, 1)
    h_far(3)
    i_ring(3, 2, 3)
    h_far(4)

    for yy in range(8):
        h = hb[:, yy * 16:(yy + 1) * 16, :].reshape(256, 256).astype(BF16)
        hst[yy, 0:384, :] = lax.dot_general(pick0, h, NT, preferred_element_type=F32).astype(BF16)
        hst[yy, 384:512, :] = lax.dot_general(pick1, h, NT, preferred_element_type=F32).astype(BF16)

    acc[...] = jnp.zeros_like(acc)

    def tokens(yy):
        for g in range(4):
            arrived(chunk(1 - c, yy, g), rsc.at[yy, g])
        w0 = ib[0, yy].reshape(256, 256).astype(BF16)
        w1 = ib[1, yy].reshape(256, 256).astype(BF16)
        acc[0:384, :] += jnp.dot(hst[yy, 0:384, :], w0, preferred_element_type=F32)
        acc[384:512, :] += jnp.dot(hst[yy, 384:512, :], w1, preferred_element_type=F32)

    tokens(y)
    for n in range(1, 4):
        tokens(lax.rem(y + n, 8))
        tokens(lax.rem(y + 8 - n, 8))
    i_ring(4, 0, 1, 2, 3)
    tokens(lax.rem(y + 4, 8))

    for half in range(2):
        g0 = acc[0:384, half * 128:(half + 1) * 128].reshape(16, 24, 128)
        g1 = acc[384:512, half * 128:(half + 1) * 128].reshape(16, 8, 128)
        gs[:, half * 32:half * 32 + 24, :] = g0
        gs[:, half * 32 + 24:half * 32 + 32, :] = g1
        q0 = jnp.sum(jnp.sum((g0 * g0).reshape(16, 3, 8, 128), axis=0), axis=1)
        q1 = jnp.sum(jnp.sum(g1 * g1, axis=0), axis=0, keepdims=True)
        q = jnp.concatenate([q0, q1], axis=0)
        gs[:, 64 + half * 4:68 + half * 4, :] = jnp.broadcast_to(q[None], (16, 4, 128))

    for i, n in enumerate((4, 3, 5, 2, 6, 1, 7, 0)):
        d = far(n)
        send(gs.at[d], rb.at[dp], ssg.at[i], rsg.at[dp], (d, shard))
    for i, n in enumerate((4, 3, 5, 2, 6, 1, 7)):
        d = near(n)
        send(gs.at[d], rb.at[dp], ssg.at[8 + i], rsg.at[dp], (d, shard))
    keep = [
        pltpu.make_async_copy(gs.at[dp], rb.at[dp], loc.at[2]),
        pltpu.make_async_copy(sown, sb.at[dp], loc.at[3]),
    ]
    for cp in keep:
        cp.start()
    for d in peers:
        arrived(sb.at[d], rss.at[d])
    for d in peers:
        arrived(rb.at[d], rsg.at[d])
    for cp in keep:
        cp.wait()
    for cp in sent:
        cp.wait_send()


def finish(rb, sb, owners, states, params, cols, out_p, out_r, out_c):
    live, row_st, eye = own_slots(row_keys(owners[...]), lax.axis_index("dp"), states[...])
    slot8 = lax.broadcasted_iota(jnp.int32, (32, 128), 0) >> 3
    lane = lax.broadcasted_iota(jnp.int32, (32, 128), 1)
    sq = jnp.zeros((32, 128), F32)
    cs = jnp.zeros((4, 128), F32)
    for d in range(16):
        for half in range(2):
            g = rb[d, half * 32:half * 32 + 32, :]
            sq = sq + g * g
            cs = cs + rb[d, 64 + half * 4:68 + half * 4, :]
    row_val = 0.5 * row_st + 0.5 * (jnp.sum(sq, axis=1, keepdims=True) / 4096.0 + EPS_SQUARE)
    cs = cs + 64.0 * 32.0 * EPS_SQUARE
    all_cs = jnp.sum(jnp.broadcast_to(cs[:, None, :], (4, 8, 128)).reshape(32, 128), axis=1, keepdims=True)
    all_sb = jnp.sum(sb[...], axis=0)
    all_st = jnp.sum(jnp.where(lane == slot8 * 32, all_sb, 0.0), axis=1, keepdims=True)
    row_mean = (0.5 * all_st + 0.5 * (all_cs / 4096.0)) / 64.0
    by_row = 0.5 * lax.rsqrt(row_val / row_mean)
    out_r[...] = jnp.sum(jnp.where(eye, row_val * live, 0.0), axis=0, keepdims=True)
    for d in range(16):
        for half in range(2):
            at = d * 256 + half * 128
            q = rb[d, 64 + half * 4:68 + half * 4, :]
            new_col = 0.5 * cols[:, at:at + 128] + 0.5 * (q + 64.0 * EPS_SQUARE) / 64.0
            out_c[:, at:at + 128] = new_col
            by_col = jnp.broadcast_to(lax.rsqrt(new_col)[:, None, :], (4, 8, 128)).reshape(32, 128)
            g = rb[d, half * 32:half * 32 + 32, :]
            par = params[:, at:at + 128].astype(F32)
            out_p[:, at:at + 128] = ((par - g * by_row * by_col) * live).astype(BF16)


def on_device(head_terms, inputs, owner_list, param_slots, row_state, col_state):
    vm = pl.BlockSpec(memory_space=pltpu.VMEM)
    hbm = pl.BlockSpec(memory_space=pl.ANY)
    dma = pltpu.SemaphoreType.DMA
    owners = owner_list.reshape(1, 256)
    rb, sb = pl.pallas_call(
        exchange,
        out_shape=(jax.ShapeDtypeStruct((16, 72, 128), F32), jax.ShapeDtypeStruct((16, 1, 128), F32)),
        in_specs=[hbm, hbm, vm, vm],
        out_specs=(hbm, hbm),
        scratch_shapes=[
            pltpu.VMEM((128, 256), BF16),
            pltpu.VMEM((16, 2, 4096), BF16),
            pltpu.VMEM((16, 16, 256), F32),
            pltpu.VMEM((16, 128, 256), F32),
            pltpu.VMEM((2, 8, 16, 16, 256), F32),
            pltpu.VMEM((8, 512, 256), BF16),
            pltpu.VMEM((512, 256), F32),
            pltpu.VMEM((16, 72, 128), F32),
            pltpu.VMEM((1, 128), F32),
            dma((15,)), dma((16,)),
            dma((15,)), dma((16,)),
            dma((7, 4)), dma((8, 4)),
            dma((8, 4)), dma((8, 4)),
            dma((15,)), dma((16,)),
            dma((15,)), dma((16,)),
            dma((4,)),
        ],
        compiler_params=pltpu.CompilerParams(collective_id=0, has_side_effects=True),
    )(head_terms.reshape(128, 256), inputs, owners, row_state)
    new_params, new_rows, new_cols = pl.pallas_call(
        finish,
        out_shape=(
            jax.ShapeDtypeStruct((32, 4096), BF16),
            jax.ShapeDtypeStruct((1, 32), F32),
            jax.ShapeDtypeStruct((4, 4096), F32),
        ),
        in_specs=[vm] * 6,
        out_specs=(vm, vm, vm),
    )(rb, sb, owners, row_state, param_slots.reshape(32, 4096), col_state.reshape(4, 4096))
    return (new_params[None], new_rows, new_cols[None])


def solution(mesh):
    placed = (
        P("dp", "shard", None),
        P("dp", None, None),
        P("shard", None, None),
        P("shard", "dp", None),
        P("shard", "dp"),
        P("shard", None, None),
    )
    return jax.shard_map(
        on_device,
        mesh=mesh,
        in_specs=placed,
        out_specs=(P("shard", "dp", None), P("shard", "dp"), P("shard", None, None)),
        check_vma=False,
    )
```

time: 95 us -> 83.9 us (0.88)
  local copies, waits for them, and re-layouts: 5.36 us -> 0 us
  other arithmetic: 3.2 us -> 0 us
  Pallas kernels: 84.5 us -> 83 us
    unnamed x8 -> x0, local copies, waits for them, and re-layouts: 3.79 us -> none
    convert_element_type x2 -> x0, other arithmetic: 2.57 us -> none  [the longest x1 1.72 us: on_device(): ip = jnp.transpose(piece, (1, 0, 2)).astype(F32)]
    pallas_call x1 -> x2, Pallas kernels: 84.5 us -> 83 us  [the longest x1 80.7 us: on_device(): pl.pallas_call(exchange, out_shape=(jax.ShapeDtypeStruct((16, 72, 128), F...]
    reshape x2 -> x0, local copies, waits for them, and re-layouts: 1.54 us -> none  [the longest x1 0.81 us: on_device(): owner_list.reshape(256, 1)]
where the time goes in v2:
time: 83.9 us; the launch traced here: 83.6 us
  Pallas kernels  83 us (99%)
    pallas_call x1, Pallas kernels, on_device(): pl.pallas_call(exchange, out_shape=(jax.ShapeDtypeStruct((16, 72, 128), F...  80.7 us
    pallas_call x1, Pallas kernels, on_device(): pl.pallas_call(finish, out_shape=(jax.ShapeDtypeStruct((32, 4096), BF16),...  2.27 us

profile of v2, /device:TPU:1, one launch (start us, length us, event | category | flops | bytes accessed | tf_op | source)
XLA Modules:
  0.0 83.6 jit_solution(6578900585576862870)
XLA Ops:
  0.6 80.7 %shard_map.85 = (f32[16,72,128]{2,1,0:T(8,128)}, f32[16,1,128]{2,1,0:T(1,128)}) custom-call(bf16[128,256]{1,0:T(8,128)(2,1)} %bitcast.7, bf16[128,2,4096]{2,1,0:T(2,128)(2,1)} %inputs.1, s32[1,256]{1,0:T(1,128)} %bitcast.9, f32[1,32]{1,0:T(1,128)} %states.3), custom_call_target="tpu_custom_call" | custom-call | tf_op jit(solution)/shard_map/pallas_call | solution.py:308
  81.3 2.3 %shard_map.86 = (bf16[32,4096]{1,0:T(8,128)(2,1)}, f32[1,32]{1,0:T(1,128)}, f32[4,4096]{1,0:T(4,128)}) custom-call(f32[16,72,128]{2,1,0:T(8,128)} %get-tuple-element.8.rb, f32[16,1,128]{2,1,0:T(1,128)} %get-tuple-element.9.sb, s32[1,256]{1,0:T(1,128)} %bitcast.10, f32[1,32]{1,0:T(1,128)} %states.3, bf16[32,4096]{1,0:T(8,128)(2,1)} %bitcast.6, f32[4,4096]{1,0:T(4,128)} %bitcast.8), custom_call_target="tpu_custom_call" | custom-call | tf_op jit(solution)/shard_map/pallas_call | solution.py:333

commit v3 on v2

--- a/solution.py
+++ b/solution.py
@@ -38,7 +38,7 @@
 
 
 def exchange(heads, inputs, owners, states, rb, sb,
-             hraw, iraw, ipf, hb, ib, hst, acc, gs, sown,
+             hraw, iraw, ipf, hb, ib, hst, ibf, acc, gs, sown,
              ssh, rsh, ssi, rsi, ssy, rsy, ssc, rsc, sss, rss, ssg, rsg, loc):
     dp, a, z, shard, xl, y, c = place()
     other = 1 - a
@@ -72,15 +72,15 @@
     for cp in local:
         cp.start()
 
+    local[1].wait()
+    hb[dp] = hraw[...].astype(F32)
     local[0].wait()
     which = lax.broadcasted_iota(jnp.int32, (16, 2, 256), 1) == c
 
-    for d in range(16):
-        pair = iraw[:, :, d * 256:(d + 1) * 256].astype(F32)
-        ipf[d] = jnp.sum(jnp.where(which, pair, 0.0), axis=1)
-    ib[c, y, dp] = ipf[dp]
-    local[1].wait()
-    hb[dp] = hraw[...].astype(F32)
+    def widen(d):
+        at = pl.ds(pl.multiple_of(d * 256, 256), 256)
+        ipf[d] = jnp.sum(jnp.where(which, iraw[:, :, at].astype(F32), 0.0), axis=1)
+
     pl.semaphore_wait(barrier, len(greeted))
 
     sent = []
@@ -97,19 +97,29 @@
 
     count = [0]
 
-    def send_h(d, who):
-        send(hb.at[d], hb.at[d], ssh.at[count[0]], rsh.at[d], who)
+    def piece(d, p):
+        return hb.at[d, pl.ds(64 * p, 64)]
+
+    def send_h(d, p, who):
+        send(piece(d, p), piece(d, p), ssh.at[count[0]], rsh.at[d, p], who)
         count[0] += 1
 
+    for p in range(2):
+        send_h(dp, p, (far(0), shard))
+    for i, n in enumerate((1, 7, 2, 6, 3, 5, 4)):
+        d = near(n)
+        widen(d)
+        send(ipf.at[d], ib.at[c, y, dp], ssi.at[i], rsi.at[dp], (d, shard))
+    for p in range(2):
+        send_h(dp, p, right)
+        send_h(dp, p, left)
     for i, n in enumerate((4, 3, 5, 2, 6, 1, 7, 0)):
         d = far(n)
+        widen(d)
         send(ipf.at[d], ib.at[c, y, dp], ssi.at[7 + i], rsi.at[dp], (d, far_shard))
-    for i, n in enumerate((4, 3, 5, 2, 6, 1, 7)):
-        d = near(n)
-        send(ipf.at[d], ib.at[c, y, dp], ssi.at[i], rsi.at[dp], (d, shard))
-    send_h(dp, (far(0), shard))
-    send_h(dp, right)
-    send_h(dp, left)
+
+    widen(dp)
+    ib[c, y, dp] = ipf[dp]
 
     key = row_keys(owners[...])
     k0 = lax.broadcasted_iota(jnp.int32, (16, 24, 1), 0) * 32 + lax.broadcasted_iota(jnp.int32, (16, 24, 1), 1)
@@ -123,8 +133,18 @@
     for i, d in enumerate(peers):
         send(sown, sb.at[dp], sss.at[i], rss.at[dp], (d, shard))
 
-    def got_h(d):
-        arrived(hb.at[d], rsh.at[d])
+    def got_h(d, p):
+        arrived(piece(d, p), rsh.at[d, p])
+
+    def pick_h(d):
+        at = pl.ds(pl.multiple_of(d * 128, 128), 128)
+        h = hb[d].astype(BF16)
+        hst[0:384, at] = lax.dot_general(pick0, h, NT, preferred_element_type=F32).astype(BF16)
+        hst[384:512, at] = lax.dot_general(pick1, h, NT, preferred_element_type=F32).astype(BF16)
+
+    def narrow(core, yy, g):
+        at = pl.ds(4 * quads[g], 4)
+        ibf[core, at, yy] = ib[core, yy, at].astype(BF16)
 
     quads = (dp // 4, a * 2 + 1 - z // 4, other * 2 + z // 4, other * 2 + 1 - z // 4)
 
@@ -144,59 +164,77 @@
         return lax.rem(y + n - 2 * n * c + 8, 8)
 
     def h_own(s):
-        d = near(8 - s)
-        got_h(d)
+        d, e = near(8 - s), near(s)
+        for p in range(2):
+            got_h(d, p)
+            if s < 4:
+                send_h(d, p, right)
+                got_h(e, p)
+                if s < 3:
+                    send_h(e, p, left)
+        pick_h(d)
         if s < 4:
-            send_h(d, right)
-        if s < 4:
-            d = near(s)
-            got_h(d)
-            if s < 3:
-                send_h(d, left)
+            pick_h(e)
 
     def h_far(s):
-        if s == 0:
-            got_h(far(0))
-            send_h(far(0), right)
-            send_h(far(0), left)
-            return
-        if s < 4:
-            d = far(8 - s)
-            got_h(d)
-            if s < 3:
-                send_h(d, right)
-        d = far(s)
-        got_h(d)
-        if s < 4:
-            send_h(d, left)
+        d, e = far(8 - s), far(s)
+        for p in range(2):
+            if 0 < s < 4:
+                got_h(d, p)
+                if s < 3:
+                    send_h(d, p, right)
+            got_h(e, p)
+            if s == 0:
+                send_h(e, p, right)
+            if s < 4:
+                send_h(e, p, left)
+        if 0 < s < 4:
+            pick_h(d)
+        pick_h(e)
 
     def i_ring(s, *groups):
         for g in groups:
             if s == 0:
-                if g == 0:
-                    for k in range(1, 4):
-                        d = dp - z % 4 + lax.rem(z + k, 4)
-                        arrived(ib.at[c, y, d], rsi.at[d])
-                else:
-                    for k in range(4):
-                        d = 4 * quads[g] + k
-                        arrived(ib.at[c, y, d], rsi.at[d])
+                for k in range(1 if g == 0 else 0, 4):
+                    d = dp - z % 4 + lax.rem(z + k, 4) if g == 0 else 4 * quads[g] + k
+                    arrived(ib.at[c, y, d], rsi.at[d])
                 send_y(y, g, 0, fwd_shard)
                 send_y(y, g, 1, back_shard)
                 send_c(y, g, 0)
+                narrow(c, y, g)
                 continue
-            yy = upstream(s)
-            arrived(chunk(c, yy, g), rsy.at[yy, g])
+            up = upstream(s)
+            arrived(chunk(c, up, g), rsy.at[up, g])
             if s < 4:
-                send_y(yy, g, 2 * s, fwd_shard)
-            send_c(yy, g, 2 * s - 1)
+                send_y(up, g, 2 * s, fwd_shard)
+            send_c(up, g, 2 * s - 1)
             if s < 4:
-                yy = downstream(s)
-                arrived(chunk(c, yy, g), rsy.at[yy, g])
+                down = downstream(s)
+                arrived(chunk(c, down, g), rsy.at[down, g])
                 if s < 3:
-                    send_y(yy, g, 2 * s + 1, back_shard)
-                send_c(yy, g, 2 * s)
-
+                    send_y(down, g, 2 * s + 1, back_shard)
+                send_c(down, g, 2 * s)
+                narrow(c, down, g)
+            narrow(c, up, g)
+
+    def tokens(g):
+        for n in range(8):
+            yy = lax.rem(y + n, 8)
+            arrived(chunk(1 - c, yy, g), rsc.at[yy, g])
+            narrow(1 - c, yy, g)
+        at = pl.ds(pl.multiple_of(quads[g] * 512, 512), 512)
+        w0 = ibf[0, pl.ds(4 * quads[g], 4)].reshape(512, 256)
+        w1 = ibf[1, pl.ds(4 * quads[g], 4)].reshape(512, 256)
+        g0 = jnp.dot(hst[0:384, at], w0, preferred_element_type=F32)
+        g1 = jnp.dot(hst[384:512, at], w1, preferred_element_type=F32)
+        if g == 0:
+            acc[0:384, :] = g0
+            acc[384:512, :] = g1
+        else:
+            acc[0:384, :] += g0
+            acc[384:512, :] += g1
+
+    pick_h(dp)
     h_own(1)
     i_ring(0, 0, 1)
     h_far(0)
@@ -213,29 +251,13 @@
     i_ring(3, 0, 1)
     h_far(3)
     i_ring(3, 2, 3)
+    i_ring(4, 0, 1)
+    tokens(0)
+    tokens(1)
     h_far(4)
-
-    for yy in range(8):
-        h = hb[:, yy * 16:(yy + 1) * 16, :].reshape(256, 256).astype(BF16)
-        hst[yy, 0:384, :] = lax.dot_general(pick0, h, NT, preferred_element_type=F32).astype(BF16)
-        hst[yy, 384:512, :] = lax.dot_general(pick1, h, NT, preferred_element_type=F32).astype(BF16)
-
-    acc[...] = jnp.zeros_like(acc)
-
-    def tokens(yy):
-        for g in range(4):
-            arrived(chunk(1 - c, yy, g), rsc.at[yy, g])
-        w0 = ib[0, yy].reshape(256, 256).astype(BF16)
-        w1 = ib[1, yy].reshape(256, 256).astype(BF16)
-        acc[0:384, :] += jnp.dot(hst[yy, 0:384, :], w0, preferred_element_type=F32)
-        acc[384:512, :] += jnp.dot(hst[yy, 384:512, :], w1, preferred_element_type=F32)
-
-    tokens(y)
-    for n in range(1, 4):
-        tokens(lax.rem(y + n, 8))
-        tokens(lax.rem(y + 8 - n, 8))
-    i_ring(4, 0, 1, 2, 3)
-    tokens(lax.rem(y + 4, 8))
+    i_ring(4, 2, 3)
+    tokens(2)
+    tokens(3)
 
     for half in range(2):
         g0 = acc[0:384, half * 128:(half + 1) * 128].reshape(16, 24, 128)
@@ -316,11 +338,12 @@
             pltpu.VMEM((16, 16, 256), F32),
             pltpu.VMEM((16, 128, 256), F32),
             pltpu.VMEM((2, 8, 16, 16, 256), F32),
-            pltpu.VMEM((8, 512, 256), BF16),
+            pltpu.VMEM((512, 2048), BF16),
+            pltpu.VMEM((2, 16, 8, 16, 256), BF16),
             pltpu.VMEM((512, 256), F32),
             pltpu.VMEM((16, 72, 128), F32),
             pltpu.VMEM((1, 128), F32),
-            dma((15,)), dma((16,)),
+            dma((30,)), dma((16, 2)),
             dma((15,)), dma((16,)),
             dma((7, 4)), dma((8, 4)),
             dma((8, 4)), dma((8, 4)),

time: 83.9 us -> 83.2 us (level)
  no operation moved by 1% of the time
where the time goes in v3:
time: 83.2 us; the launch traced here: 83 us
  Pallas kernels  82.3 us (99%)
    pallas_call x1, Pallas kernels, on_device(): pl.pallas_call(exchange, out_shape=(jax.ShapeDtypeStruct((16, 72, 128), F...  80.1 us
    pallas_call x1, Pallas kernels, on_device(): pl.pallas_call(finish, out_shape=(jax.ShapeDtypeStruct((32, 4096), BF16),...  2.27 us

profile of v3, /device:TPU:1, one launch (start us, length us, event | category | flops | bytes accessed | tf_op | source)
XLA Modules:
  0.0 83.0 jit_solution(17649651477784566973)
XLA Ops:
  0.6 80.1 %shard_map.85 = (f32[16,72,128]{2,1,0:T(8,128)}, f32[16,1,128]{2,1,0:T(1,128)}) custom-call(bf16[128,256]{1,0:T(8,128)(2,1)} %bitcast.7, bf16[128,2,4096]{2,1,0:T(2,128)(2,1)} %inputs.1, s32[1,256]{1,0:T(1,128)} %bitcast.9, f32[1,32]{1,0:T(1,128)} %states.3), custom_call_target="tpu_custom_call" | custom-call | tf_op jit(solution)/shard_map/pallas_call | solution.py:330
  80.7 2.3 %shard_map.86 = (bf16[32,4096]{1,0:T(8,128)(2,1)}, f32[1,32]{1,0:T(1,128)}, f32[4,4096]{1,0:T(4,128)}) custom-call(f32[16,72,128]{2,1,0:T(8,128)} %get-tuple-element.8.rb, f32[16,1,128]{2,1,0:T(1,128)} %get-tuple-element.9.sb, s32[1,256]{1,0:T(1,128)} %bitcast.10, f32[1,32]{1,0:T(1,128)} %states.3, bf16[32,4096]{1,0:T(8,128)(2,1)} %bitcast.6, f32[4,4096]{1,0:T(4,128)} %bitcast.8), custom_call_target="tpu_custom_call" | custom-call | tf_op jit(solution)/shard_map/pallas_call | solution.py:356

commit v4 on v3

--- a/solution.py
+++ b/solution.py
@@ -37,8 +37,8 @@
     return live, row_st, eye
 
 
-def exchange(heads, inputs, owners, states, rb, sb,
-             hraw, iraw, ipf, hb, ib, hst, ibf, acc, gs, sown,
+def exchange(heads, inputs, owners_in, states_in, rb, sb,
+             owners, states, hraw, iraw, ipf, hb, ib, hst, ibf, acc, gs, sown,
              ssh, rsh, ssi, rsi, ssy, rsy, ssc, rsc, sss, rss, ssg, rsg, loc):
     dp, a, z, shard, xl, y, c = place()
     other = 1 - a
@@ -68,6 +68,8 @@
     local = [
         pltpu.make_async_copy(inputs.at[pl.ds(16 * y, 16)], iraw, loc.at[0]),
         pltpu.make_async_copy(heads, hraw, loc.at[1]),
+        pltpu.make_async_copy(owners_in, owners, loc.at[4]),
+        pltpu.make_async_copy(states_in, states, loc.at[5]),
     ]
     for cp in local:
         cp.start()
@@ -121,6 +123,8 @@
     widen(dp)
     ib[c, y, dp] = ipf[dp]
 
+    local[2].wait()
+    local[3].wait()
     key = row_keys(owners[...])
     k0 = lax.broadcasted_iota(jnp.int32, (16, 24, 1), 0) * 32 + lax.broadcasted_iota(jnp.int32, (16, 24, 1), 1)
     k1 = lax.broadcasted_iota(jnp.int32, (16, 8, 1), 0) * 32 + 24 + lax.broadcasted_iota(jnp.int32, (16, 8, 1), 1)
@@ -330,9 +334,11 @@
     rb, sb = pl.pallas_call(
         exchange,
         out_shape=(jax.ShapeDtypeStruct((16, 72, 128), F32), jax.ShapeDtypeStruct((16, 1, 128), F32)),
-        in_specs=[hbm, hbm, vm, vm],
+        in_specs=[hbm] * 4,
         out_specs=(hbm, hbm),
         scratch_shapes=[
+            pltpu.VMEM((1, 256), jnp.int32),
+            pltpu.VMEM((1, 32), F32),
             pltpu.VMEM((128, 256), BF16),
             pltpu.VMEM((16, 2, 4096), BF16),
             pltpu.VMEM((16, 16, 256), F32),
@@ -349,7 +355,7 @@
             dma((8, 4)), dma((8, 4)),
             dma((15,)), dma((16,)),
             dma((15,)), dma((16,)),
-            dma((4,)),
+            dma((6,)),
         ],
         compiler_params=pltpu.CompilerParams(collective_id=0, has_side_effects=True),
     )(head_terms.reshape(128, 256), inputs, owners, row_state)

time: 83.2 us -> 83 us (level)
  no operation moved by 1% of the time
where the time goes in v4:
time: 83 us; the launch traced here: 82.8 us
  Pallas kernels  82.1 us (99%)
    pallas_call x1, Pallas kernels, on_device(): pl.pallas_call(exchange, out_shape=(jax.ShapeDtypeStruct((16, 72, 128), F...  79.9 us
    pallas_call x1, Pallas kernels, on_device(): pl.pallas_call(finish, out_shape=(jax.ShapeDtypeStruct((32, 4096), BF16),...  2.27 us

profile of v4, /device:TPU:1, one launch (start us, length us, event | category | flops | bytes accessed | tf_op | source)
XLA Modules:
  0.0 82.8 jit_solution(7636126819368086552)
XLA Ops:
  0.6 79.9 %shard_map.85 = (f32[16,72,128]{2,1,0:T(8,128)}, f32[16,1,128]{2,1,0:T(1,128)}) custom-call(bf16[128,256]{1,0:T(8,128)(2,1)} %bitcast.7, bf16[128,2,4096]{2,1,0:T(2,128)(2,1)} %inputs.1, s32[1,256]{1,0:T(1,128)} %bitcast.9, f32[1,32]{1,0:T(1,128)} %states.1), custom_call_target="tpu_custom_call" | custom-call | tf_op jit(solution)/shard_map/pallas_call | solution.py:334
  80.5 2.3 %shard_map.86 = (bf16[32,4096]{1,0:T(8,128)(2,1)}, f32[1,32]{1,0:T(1,128)}, f32[4,4096]{1,0:T(4,128)}) custom-call(f32[16,72,128]{2,1,0:T(8,128)} %get-tuple-element.8.rb, f32[16,1,128]{2,1,0:T(1,128)} %get-tuple-element.9.sb, s32[1,256]{1,0:T(1,128)} %bitcast.10, f32[1,32]{1,0:T(1,128)} %states.1, bf16[32,4096]{1,0:T(8,128)(2,1)} %bitcast.6, f32[4,4096]{1,0:T(4,128)} %bitcast.8), custom_call_target="tpu_custom_call" | custom-call | tf_op jit(solution)/shard_map/pallas_call | solution.py:362
